TPU v7x, 128 devices: a whole 4x4x4 slice. The times are simulated.
128 devices in a mesh: group: 16 (over y, z), fold: 8 (over x, core).
Axes of the slice: x: 4, y: 4, z: 4, core: 2. Of those that a mesh axis runs over, the one named last changes fastest.
Arguments:
- right_side: float32 [16, 262144], P(None, ('group', 'fold')), may hold values from -6 to 6
- initial: float32 [16, 262144], P(None, ('group', 'fold')), may hold values from -6 to 6
- counts: int32 [16, 8], P('group'), may hold values from 1 to 2048, 8192 in all within a row
- columns: int32 [1024, 5], P('group'), may hold values from 0 to 69, as said below
- blocks: float32 [1024, 5, 128, 128], P('group')
Outputs:
- smoothed: float32 [16, 262144], P(None, ('group', 'fold'))
Inputs may be any that keep to these rules, and one draw needn't show every extreme that they name: Every row of counts sums to 8192, and its largest entry is 2048. `columns`: index j of row block g * 64 + i names block g * 64 + j - 3; the 5 indices of a row block are distinct and lie within 3 of i + 3.
All inputs are finite; a program needn't handle non-finite values.
Results may differ from a plain program's by a relative error of at most 0.0001.
Values sent between devices are 32-bit elements; how exact they have to be, the bound alone decides.
A program may use at most 192 MiB of HBM per device.

v0:
```python
import jax
import jax.numpy as jnp
from jax import lax
from jax.sharding import PartitionSpec as P

HB = 3
SWEEPS = 3
DEGREE = 4
upper_bound = 4.5
lower_bound = 1.35


def padded_2(shard, sides, width):
    for axis, dim in sides:
        devices, length = (lax.axis_size(axis), shard.shape[dim])
        up = [(i, (i + 1) % devices) for i in range(devices - 1)]
        down = [(j, i) for i, j in up]
        last = lax.slice_in_dim(shard, length - width, length, axis=dim)
        initial = lax.slice_in_dim(shard, 0, width, axis=dim)
        before = lax.ppermute(last, axis, up)
        after = lax.ppermute(initial, axis, down)
        shard = jnp.concatenate([before, shard, after], axis=dim)
    return shard


def on_device(right_side, initial, counts, columns, blocks):
    folds = lax.axis_size("fold")
    vectors, capacity = right_side.shape
    own_blocks, width = (blocks.shape[0], blocks.shape[2])
    live_rows = counts[0]
    starts = jnp.cumsum(live_rows) - live_rows
    stacked = jnp.stack([right_side, initial])
    gathered = lax.all_gather(stacked, "fold", axis=2, tiled=True)
    position = lax.axis_index("fold")
    row_ids = jnp.arange(own_blocks * width, dtype=jnp.int32)
    covered = starts[None, :] <= row_ids[:, None]
    owner_slot = jnp.sum(covered.astype(jnp.int32), axis=1) - 1
    row_start = jnp.max(jnp.where(covered, starts[None, :], 0), axis=1)
    source = owner_slot * capacity + row_ids - row_start
    owned = jnp.take(gathered, source, axis=2)
    target = owned[0]
    iterate = owned[1]

    def operate(vector):
        extended = padded_2(vector, (("group", 1),), HB * width)
        extended = extended.reshape(vectors, own_blocks + 2 * HB, width)
        picked = jnp.take(extended, columns, axis=1)
        result = jnp.einsum("nikc,ikrc->nir", picked, blocks, precision=lax.Precision.HIGHEST)
        return result.reshape(vectors, own_blocks * width)

    theta = (upper_bound + lower_bound) / 2.0
    delta = (upper_bound - lower_bound) / 2.0
    for sweep in range(SWEEPS):
        resid = target - operate(iterate)
        update = resid / theta
        ratio_now = delta / theta
        for step in range(DEGREE):
            iterate = iterate + update
            if step + 1 < DEGREE:
                resid = resid - operate(update)
                ratio_next = 1.0 / (2.0 * theta / delta - ratio_now)
                update = ratio_next * ratio_now * update + 2.0 * ratio_next / delta * resid
                ratio_now = ratio_next
    fold_ids = jnp.arange(folds, dtype=jnp.int32)
    my_start = jnp.sum(jnp.where(fold_ids == position, starts, 0))
    my_count = jnp.sum(jnp.where(fold_ids == position, live_rows, 0))
    padded = jnp.concatenate([iterate, jnp.zeros((vectors, capacity), jnp.float32)], axis=1)
    piece = lax.dynamic_slice_in_dim(padded, my_start, capacity, 1)
    valid = jnp.arange(capacity, dtype=jnp.int32) < my_count
    return jnp.where(valid[None, :], piece, jnp.float32(0.0))


def solution(mesh):
    placed = (
        P(None, ("group", "fold")),
        P(None, ("group", "fold")),
        P("group", None),
        P("group", None),
        P("group", None, None, None),
    )
    return jax.shard_map(
        on_device, mesh=mesh, in_specs=placed, out_specs=P(None, ("group", "fold")), check_vma=False
    )
```

profile of v0, /device:TPU:8, one launch (start us, length us, event | category | flops | bytes accessed | tf_op | source)
XLA Modules:
  0.0 559.2 jit_solution(11467768197865809706)
XLA Ops:
  11.8 24.7 %all-gather.2.cloned.1.call-done = f32[2,16,16384]{2,1,0:T(8,128)} async-done(((f32[2,16,2048]{2,1,0:T(8,128)}), f32[2,16,16384]{2,1,0:T(8,128)}) %all-gather.2.cloned.1.call-update) | async-done | bytes 2097168 | tf_op jit(solution)/shard_map/all_gather | solution.py:33
  36.5 18.6 %copy.304 = f32[2,16,16384]{1,0,2:T(2,128)} copy(f32[2,16,16384]{2,1,0:T(8,128)} %all-gather.2.cloned.1.call-done) | data formatting | bytes 4194304 | tf_op jit(solution)/shard_map/all_gather | solution.py:33
  55.2 62.3 %gather_fusion = f32[8192,2,16]{2,1,0:T(2,128)} fusion(f32[2,16,16384]{1,0,2:T(2,128)} %copy.304, s32[8192]{0:T(1024)S(1)} %broadcast_clamp_fusion), kind=kCustom, calls=%fused_computation.12 | custom fusion | bytes 2129920 | tf_op jit(solution)/shard_map/jit(_take)/gather | solution.py:40
  117.4 9.3 %copy.305 = f32[8192,2,16]{0,2,1:T(8,128)S(1)} copy(f32[8192,2,16]{2,1,0:T(2,128)} %gather_fusion) | data formatting | bytes 2097152 | tf_op jit(solution)/shard_map/jit(_take)/gather | solution.py:40
  138.3 23.1 %fusion.60 = f32[64,2,8,128]{3,2,1,0:T(8,128)S(1)} fusion(f32[64,5,128,128]{3,2,1,0:T(8,128)} %param.11, f32[64,5,16,128]{3,2,1,0:T(8,128)S(1)} %bitcast.334, pred[64,5]{1,0:T(8,128)(4,1)S(1)} %copy.306), kind=kOutput, calls=%fused_computation.73 | convolution fusion | flops 1007288320 | bytes 24117568 | tf_op jit(solution)/shard_map/nikc,ikrc->nir/dot_general | solution.py:48
  165.6 5.3 collective-permute-start.3
  174.1 23.1 %fusion.63 = f32[64,2,8,128]{3,2,1,0:T(8,128)S(1)} fusion(f32[64,5,128,128]{3,2,1,0:T(8,128)} %param.11, f32[64,5,16,128]{3,2,1,0:T(8,128)S(1)} %bitcast.335, pred[64,5]{1,0:T(8,128)(4,1)S(1)} %copy.306), kind=kOutput, calls=%fused_computation.74 | convolution fusion | flops 1007288320 | bytes 24117568 | tf_op jit(solution)/shard_map/nikc,ikrc->nir/dot_general | solution.py:48
  200.9 4.6 collective-permute-start.5
  209.0 23.1 %fusion.66 = f32[64,2,8,128]{3,2,1,0:T(8,128)S(1)} fusion(f32[64,5,128,128]{3,2,1,0:T(8,128)} %param.11, f32[64,5,16,128]{3,2,1,0:T(8,128)S(1)} %bitcast.336, pred[64,5]{1,0:T(8,128)(4,1)S(1)} %copy.306), kind=kOutput, calls=%fused_computation.75 | convolution fusion | flops 1007288320 | bytes 24117568 | tf_op jit(solution)/shard_map/nikc,ikrc->nir/dot_general | solution.py:48
  236.0 5.2 collective-permute-start.7
  244.1 23.2 %fusion.69 = f32[64,2,8,128]{3,2,1,0:T(8,128)S(1)} fusion(f32[64,5,128,128]{3,2,1,0:T(8,128)} %param.11, f32[64,5,16,128]{3,2,1,0:T(8,128)S(1)} %bitcast.337, pred[64,5]{1,0:T(8,128)(4,1)S(1)} %copy.306), kind=kOutput, calls=%fused_computation.76 | convolution fusion | flops 1007288320 | bytes 24117568 | tf_op jit(solution)/shard_map/nikc,ikrc->nir/dot_general | solution.py:48
  271.3 4.6 collective-permute-start.9
  279.4 23.1 %fusion.72 = f32[64,2,8,128]{3,2,1,0:T(8,128)S(1)} fusion(f32[64,5,128,128]{3,2,1,0:T(8,128)} %param.11, f32[64,5,16,128]{3,2,1,0:T(8,128)S(1)} %bitcast.338, pred[64,5]{1,0:T(8,128)(4,1)S(1)} %copy.306), kind=kOutput, calls=%fused_computation.77 | convolution fusion | flops 1007288320 | bytes 24117568 | tf_op jit(solution)/shard_map/nikc,ikrc->nir/dot_general | solution.py:48
  307.0 4.8 collective-permute-start.11
  315.1 23.1 %fusion.75 = f32[64,2,8,128]{3,2,1,0:T(8,128)S(1)} fusion(f32[64,5,128,128]{3,2,1,0:T(8,128)} %param.11, f32[64,5,16,128]{3,2,1,0:T(8,128)S(1)} %bitcast.339, pred[64,5]{1,0:T(8,128)(4,1)S(1)} %copy.306), kind=kOutput, calls=%fused_computation.78 | convolution fusion | flops 1007288320 | bytes 24117568 | tf_op jit(solution)/shard_map/nikc,ikrc->nir/dot_general | solution.py:48
  350.0 23.1 %fusion.78 = f32[64,2,8,128]{3,2,1,0:T(8,128)S(1)} fusion(f32[64,5,128,128]{3,2,1,0:T(8,128)} %param.11, f32[64,5,16,128]{3,2,1,0:T(8,128)S(1)} %bitcast.340, pred[64,5]{1,0:T(8,128)(4,1)S(1)} %copy.306), kind=kOutput, calls=%fused_computation.79 | convolution fusion | flops 1007288320 | bytes 24117568 | tf_op jit(solution)/shard_map/nikc,ikrc->nir/dot_general | solution.py:48
  377.0 4.8 collective-permute-start.15
  385.1 23.2 %fusion.81 = f32[64,2,8,128]{3,2,1,0:T(8,128)S(1)} fusion(f32[64,5,128,128]{3,2,1,0:T(8,128)} %param.11, f32[64,5,16,128]{3,2,1,0:T(8,128)S(1)} %bitcast.341, pred[64,5]{1,0:T(8,128)(4,1)S(1)} %copy.306), kind=kOutput, calls=%fused_computation.80 | convolution fusion | flops 1007288320 | bytes 24117568 | tf_op jit(solution)/shard_map/nikc,ikrc->nir/dot_general | solution.py:48
  420.4 23.1 %fusion.84 = f32[64,2,8,128]{3,2,1,0:T(8,128)S(1)} fusion(f32[64,5,128,128]{3,2,1,0:T(8,128)} %param.11, f32[64,5,16,128]{3,2,1,0:T(8,128)S(1)} %bitcast.342, pred[64,5]{1,0:T(8,128)(4,1)S(1)} %copy.306), kind=kOutput, calls=%fused_computation.81 | convolution fusion | flops 1007288320 | bytes 24117568 | tf_op jit(solution)/shard_map/nikc,ikrc->nir/dot_general | solution.py:48
  448.0 5.0 collective-permute-start.19
  456.1 23.1 %fusion.87 = f32[64,2,8,128]{3,2,1,0:T(8,128)S(1)} fusion(f32[64,5,128,128]{3,2,1,0:T(8,128)} %param.11, f32[64,5,16,128]{3,2,1,0:T(8,128)S(1)} %bitcast.343, pred[64,5]{1,0:T(8,128)(4,1)S(1)} %copy.306), kind=kOutput, calls=%fused_computation.82 | convolution fusion | flops 1007288320 | bytes 24117568 | tf_op jit(solution)/shard_map/nikc,ikrc->nir/dot_general | solution.py:48
  491.1 23.1 %fusion.90 = f32[64,2,8,128]{3,2,1,0:T(8,128)S(1)} fusion(f32[64,5,128,128]{3,2,1,0:T(8,128)} %param.11, f32[64,5,16,128]{3,2,1,0:T(8,128)S(1)} %bitcast.344, pred[64,5]{1,0:T(8,128)(4,1)S(1)} %copy.306), kind=kOutput, calls=%fused_computation.83 | convolution fusion | flops 1007288320 | bytes 24117568 | tf_op jit(solution)/shard_map/nikc,ikrc->nir/dot_general | solution.py:48
  518.7 4.8 collective-permute-start.23
  527.9 23.2 %fusion.93 = f32[64,2,8,128]{3,2,1,0:T(8,128)S(1)} fusion(f32[64,5,128,128]{3,2,1,0:T(8,128)} %param.11, f32[64,5,16,128]{3,2,1,0:T(8,128)S(1)} %bitcast.333, pred[64,5]{1,0:T(8,128)(4,1)S(1)} %copy.306), kind=kOutput, calls=%fused_computation.84 | convolution fusion | flops 1007288320 | bytes 24117568 | tf_op jit(solution)/shard_map/nikc,ikrc->nir/dot_general | solution.py:48
  (199 shorter events, 111.1 us)
Async XLA Ops:
  6.5 30.0 %all-gather.2.cloned.1.call-start = ((), (), s32[]{:S(2)}) async-start(), calls=%async_computation | async-start | bytes 2359296 | tf_op jit(solution)/shard_map/all_gather | solution.py:33
  126.9 8.1 %collective-permute-start = (f32[16,384]{1,0:T(8,128)S(1)}, f32[16,384]{1,0:T(8,128)S(1)}, u32[]{:S(2)}, u32[]{:S(2)}) collective-permute-start(f32[16,384]{1,0:T(8,128)S(1)} %get-tuple-element.38), channel_id=1, source_target_pairs={{0,8},{8,16},{16,24},{24,32},{32,40},{40,48},{48,56},{56,64},{64,7... | collective-permute-start | bytes 73736 | tf_op jit(solution)/shard_map/ppermute | solution.py:20
  162.4 8.5 %collective-permute-start.2 = (f32[16,384]{1,0:T(8,128)S(1)}, f32[16,384]{1,0:T(8,128)S(1)}, u32[]{:S(2)}, u32[]{:S(2)}) collective-permute-start(f32[16,384]{1,0:T(8,128)S(1)} %get-tuple-element.36), channel_id=1, source_target_pairs={{0,8},{8,16},{16,24},{24,32},{32,40},{40,48},{48,56},{56,64},{64,7... | collective-permute-start | bytes 73736 | tf_op jit(solution)/shard_map/ppermute | solution.py:20
  165.6 6.5 %collective-permute-start.3 = (f32[16,384]{1,0:T(8,128)S(1)}, f32[16,384]{1,0:T(8,128)S(1)}, u32[]{:S(2)}, u32[]{:S(2)}) collective-permute-start(f32[16,384]{1,0:T(8,128)S(1)} %get-tuple-element.37), channel_id=1, source_target_pairs={{8,0},{16,8},{24,16},{32,24},{40,32},{48,40},{56,48},{64,56},{72,6... | collective-permute-start | bytes 73736 | tf_op jit(solution)/shard_map/ppermute | solution.py:21
  197.3 8.3 %collective-permute-start.4 = (f32[16,384]{1,0:T(8,128)S(1)}, f32[16,384]{1,0:T(8,128)S(1)}, u32[]{:S(2)}, u32[]{:S(2)}) collective-permute-start(f32[16,384]{1,0:T(8,128)S(1)} %get-tuple-element.34), channel_id=1, source_target_pairs={{0,8},{8,16},{16,24},{24,32},{32,40},{40,48},{48,56},{56,64},{64,7... | collective-permute-start | bytes 73736 | tf_op jit(solution)/shard_map/ppermute | solution.py:20
  200.9 6.1 %collective-permute-start.5 = (f32[16,384]{1,0:T(8,128)S(1)}, f32[16,384]{1,0:T(8,128)S(1)}, u32[]{:S(2)}, u32[]{:S(2)}) collective-permute-start(f32[16,384]{1,0:T(8,128)S(1)} %get-tuple-element.35), channel_id=1, source_target_pairs={{8,0},{16,8},{24,16},{32,24},{40,32},{48,40},{56,48},{64,56},{72,6... | collective-permute-start | bytes 73736 | tf_op jit(solution)/shard_map/ppermute | solution.py:21
  232.4 8.8 %collective-permute-start.6 = (f32[16,384]{1,0:T(8,128)S(1)}, f32[16,384]{1,0:T(8,128)S(1)}, u32[]{:S(2)}, u32[]{:S(2)}) collective-permute-start(f32[16,384]{1,0:T(8,128)S(1)} %get-tuple-element.32), channel_id=1, source_target_pairs={{0,8},{8,16},{16,24},{24,32},{32,40},{40,48},{48,56},{56,64},{64,7... | collective-permute-start | bytes 73736 | tf_op jit(solution)/shard_map/ppermute | solution.py:20
  236.0 6.1 %collective-permute-start.7 = (f32[16,384]{1,0:T(8,128)S(1)}, f32[16,384]{1,0:T(8,128)S(1)}, u32[]{:S(2)}, u32[]{:S(2)}) collective-permute-start(f32[16,384]{1,0:T(8,128)S(1)} %get-tuple-element.33), channel_id=1, source_target_pairs={{8,0},{16,8},{24,16},{32,24},{40,32},{48,40},{56,48},{64,56},{72,6... | collective-permute-start | bytes 73736 | tf_op jit(solution)/shard_map/ppermute | solution.py:21
  267.6 8.3 %collective-permute-start.8 = (f32[16,384]{1,0:T(8,128)S(1)}, f32[16,384]{1,0:T(8,128)S(1)}, u32[]{:S(2)}, u32[]{:S(2)}) collective-permute-start(f32[16,384]{1,0:T(8,128)S(1)} %get-tuple-element.30), channel_id=1, source_target_pairs={{0,8},{8,16},{16,24},{24,32},{32,40},{40,48},{48,56},{56,64},{64,7... | collective-permute-start | bytes 73736 | tf_op jit(solution)/shard_map/ppermute | solution.py:20
  271.3 6.1 %collective-permute-start.9 = (f32[16,384]{1,0:T(8,128)S(1)}, f32[16,384]{1,0:T(8,128)S(1)}, u32[]{:S(2)}, u32[]{:S(2)}) collective-permute-start(f32[16,384]{1,0:T(8,128)S(1)} %get-tuple-element.31), channel_id=1, source_target_pairs={{8,0},{16,8},{24,16},{32,24},{40,32},{48,40},{56,48},{64,56},{72,6... | collective-permute-start | bytes 73736 | tf_op jit(solution)/shard_map/ppermute | solution.py:21
  303.4 8.4 %collective-permute-start.10 = (f32[16,384]{1,0:T(8,128)S(1)}, f32[16,384]{1,0:T(8,128)S(1)}, u32[]{:S(2)}, u32[]{:S(2)}) collective-permute-start(f32[16,384]{1,0:T(8,128)S(1)} %get-tuple-element.28), channel_id=1, source_target_pairs={{0,8},{8,16},{16,24},{24,32},{32,40},{40,48},{48,56},{56,64},{64,7... | collective-permute-start | bytes 73736 | tf_op jit(solution)/shard_map/ppermute | solution.py:20
  307.0 6.1 %collective-permute-start.11 = (f32[16,384]{1,0:T(8,128)S(1)}, f32[16,384]{1,0:T(8,128)S(1)}, u32[]{:S(2)}, u32[]{:S(2)}) collective-permute-start(f32[16,384]{1,0:T(8,128)S(1)} %get-tuple-element.29), channel_id=1, source_target_pairs={{8,0},{16,8},{24,16},{32,24},{40,32},{48,40},{56,48},{64,56},{72,6... | collective-permute-start | bytes 73736 | tf_op jit(solution)/shard_map/ppermute | solution.py:21
  338.3 8.3 %collective-permute-start.12 = (f32[16,384]{1,0:T(8,128)S(1)}, f32[16,384]{1,0:T(8,128)S(1)}, u32[]{:S(2)}, u32[]{:S(2)}) collective-permute-start(f32[16,384]{1,0:T(8,128)S(1)} %get-tuple-element.26), channel_id=1, source_target_pairs={{0,8},{8,16},{16,24},{24,32},{32,40},{40,48},{48,56},{56,64},{64,7... | collective-permute-start | bytes 73736 | tf_op jit(solution)/shard_map/ppermute | solution.py:20
  341.9 6.1 %collective-permute-start.13 = (f32[16,384]{1,0:T(8,128)S(1)}, f32[16,384]{1,0:T(8,128)S(1)}, u32[]{:S(2)}, u32[]{:S(2)}) collective-permute-start(f32[16,384]{1,0:T(8,128)S(1)} %get-tuple-element.27), channel_id=1, source_target_pairs={{8,0},{16,8},{24,16},{32,24},{40,32},{48,40},{56,48},{64,56},{72,6... | collective-permute-start | bytes 73736 | tf_op jit(solution)/shard_map/ppermute | solution.py:21
  373.4 8.5 %collective-permute-start.14 = (f32[16,384]{1,0:T(8,128)S(1)}, f32[16,384]{1,0:T(8,128)S(1)}, u32[]{:S(2)}, u32[]{:S(2)}) collective-permute-start(f32[16,384]{1,0:T(8,128)S(1)} %get-tuple-element.24), channel_id=1, source_target_pairs={{0,8},{8,16},{16,24},{24,32},{32,40},{40,48},{48,56},{56,64},{64,7... | collective-permute-start | bytes 73736 | tf_op jit(solution)/shard_map/ppermute | solution.py:20
  377.0 6.1 %collective-permute-start.15 = (f32[16,384]{1,0:T(8,128)S(1)}, f32[16,384]{1,0:T(8,128)S(1)}, u32[]{:S(2)}, u32[]{:S(2)}) collective-permute-start(f32[16,384]{1,0:T(8,128)S(1)} %get-tuple-element.25), channel_id=1, source_target_pairs={{8,0},{16,8},{24,16},{32,24},{40,32},{48,40},{56,48},{64,56},{72,6... | collective-permute-start | bytes 73736 | tf_op jit(solution)/shard_map/ppermute | solution.py:21
  408.6 8.3 %collective-permute-start.16 = (f32[16,384]{1,0:T(8,128)S(1)}, f32[16,384]{1,0:T(8,128)S(1)}, u32[]{:S(2)}, u32[]{:S(2)}) collective-permute-start(f32[16,384]{1,0:T(8,128)S(1)} %get-tuple-element.22), channel_id=1, source_target_pairs={{0,8},{8,16},{16,24},{24,32},{32,40},{40,48},{48,56},{56,64},{64,7... | collective-permute-start | bytes 73736 | tf_op jit(solution)/shard_map/ppermute | solution.py:20
  412.3 6.1 %collective-permute-start.17 = (f32[16,384]{1,0:T(8,128)S(1)}, f32[16,384]{1,0:T(8,128)S(1)}, u32[]{:S(2)}, u32[]{:S(2)}) collective-permute-start(f32[16,384]{1,0:T(8,128)S(1)} %get-tuple-element.23), channel_id=1, source_target_pairs={{8,0},{16,8},{24,16},{32,24},{40,32},{48,40},{56,48},{64,56},{72,6... | collective-permute-start | bytes 73736 | tf_op jit(solution)/shard_map/ppermute | solution.py:21
  444.4 8.7 %collective-permute-start.18 = (f32[16,384]{1,0:T(8,128)S(1)}, f32[16,384]{1,0:T(8,128)S(1)}, u32[]{:S(2)}, u32[]{:S(2)}) collective-permute-start(f32[16,384]{1,0:T(8,128)S(1)} %get-tuple-element.20), channel_id=1, source_target_pairs={{0,8},{8,16},{16,24},{24,32},{32,40},{40,48},{48,56},{56,64},{64,7... | collective-permute-start | bytes 73736 | tf_op jit(solution)/shard_map/ppermute | solution.py:20
  448.0 6.1 %collective-permute-start.19 = (f32[16,384]{1,0:T(8,128)S(1)}, f32[16,384]{1,0:T(8,128)S(1)}, u32[]{:S(2)}, u32[]{:S(2)}) collective-permute-start(f32[16,384]{1,0:T(8,128)S(1)} %get-tuple-element.21), channel_id=1, source_target_pairs={{8,0},{16,8},{24,16},{32,24},{40,32},{48,40},{56,48},{64,56},{72,6... | collective-permute-start | bytes 73736 | tf_op jit(solution)/shard_map/ppermute | solution.py:21
  479.4 8.9 %collective-permute-start.20 = (f32[16,384]{1,0:T(8,128)S(1)}, f32[16,384]{1,0:T(8,128)S(1)}, u32[]{:S(2)}, u32[]{:S(2)}) collective-permute-start(f32[16,384]{1,0:T(8,128)S(1)} %get-tuple-element.18), channel_id=1, source_target_pairs={{0,8},{8,16},{16,24},{24,32},{32,40},{40,48},{48,56},{56,64},{64,7... | collective-permute-start | bytes 73736 | tf_op jit(solution)/shard_map/ppermute | solution.py:20
  483.0 6.1 %collective-permute-start.21 = (f32[16,384]{1,0:T(8,128)S(1)}, f32[16,384]{1,0:T(8,128)S(1)}, u32[]{:S(2)}, u32[]{:S(2)}) collective-permute-start(f32[16,384]{1,0:T(8,128)S(1)} %get-tuple-element.19), channel_id=1, source_target_pairs={{8,0},{16,8},{24,16},{32,24},{40,32},{48,40},{56,48},{64,56},{72,6... | collective-permute-start | bytes 73736 | tf_op jit(solution)/shard_map/ppermute | solution.py:21
  515.1 10.8 %collective-permute-start.22 = (f32[16,384]{1,0:T(8,128)S(1)}, f32[16,384]{1,0:T(8,128)S(1)}, u32[]{:S(2)}, u32[]{:S(2)}) collective-permute-start(f32[16,384]{1,0:T(8,128)S(1)} %get-tuple-element.16), channel_id=1, source_target_pairs={{0,8},{8,16},{16,24},{24,32},{32,40},{40,48},{48,56},{56,64},{64,7... | collective-permute-start | bytes 73736 | tf_op jit(solution)/shard_map/ppermute | solution.py:20
  518.7 7.2 %collective-permute-start.23 = (f32[16,384]{1,0:T(8,128)S(1)}, f32[16,384]{1,0:T(8,128)S(1)}, u32[]{:S(2)}, u32[]{:S(2)}) collective-permute-start(f32[16,384]{1,0:T(8,128)S(1)} %get-tuple-element.17), channel_id=1, source_target_pairs={{8,0},{16,8},{24,16},{32,24},{40,32},{48,40},{56,48},{64,56},{72,6... | collective-permute-start | bytes 73736 | tf_op jit(solution)/shard_map/ppermute | solution.py:21
  (46 other events, 869.5 us)
Sparse Core Ops, SparseCore 0:
  9.0 27.4 all-gather.1
where the time goes:
time: 566 us; the launch traced here: 559 us
  matrix products  277 us (49%)
  local copies, waits for them, and re-layouts  115 us (20%)
  starting transfers between devices  100 us (18%)
  waiting for transfers between devices  38.7 us (7%)
  between operations  16.6 us (3%)
  other arithmetic  11.6 us (2%)
    dot_general x12, matrix products, operate(): jnp.einsum('nikc,ikrc->nir', picked, blocks, precision=lax.Precision.HIGH...  277 us
    gather x2, local copies, waits for them, and re-layouts, on_device(): owned = jnp.take(gathered, source, axis=2)  71.6 us
    ppermute x12, starting transfers between devices, padded_2(): after = lax.ppermute(initial, axis, down)  57.6 us
    ppermute x12, starting transfers between devices, padded_2(): before = lax.ppermute(last, axis, up)  42.8 us
    all_gather x1, waiting for transfers between devices, on_device(): gathered = lax.all_gather(stacked, 'fold', axis=2, tiled=True)  24.7 us
    gather x12, local copies, waits for them, and re-layouts, operate(): picked = jnp.take(extended, columns, axis=1)  22.7 us
    all_gather x1, local copies, waits for them, and re-layouts, on_device(): gathered = lax.all_gather(stacked, 'fold', axis=2, tiled=True)  18.6 us
    ppermute x12, waiting for transfers between devices, padded_2(): after = lax.ppermute(initial, axis, down)  14 us
  transfers between devices with their start and end apart: 25, of which 12 were waited for; matrix products, arithmetic and copies ran while one was open for 1% of the time, Pallas kernels for 0%

commit v1 on v0

--- a/solution.py
+++ b/solution.py
@@ -8,6 +8,15 @@
 DEGREE = 4
 upper_bound = 4.5
 lower_bound = 1.35
+
+
+def pack_panels_by_axis(a0, array_dim):
+    a0 = jnp.moveaxis(a0, 0, array_dim)
+    q_next = a0.shape
+    finding = a0.reshape(
+        *q_next[:array_dim], q_next[array_dim] * q_next[array_dim + 1], *q_next[array_dim + 2 :]
+    )
+    return finding
 
 
 def padded_2(shard, sides, width):
@@ -30,7 +39,21 @@
     live_rows = counts[0]
     starts = jnp.cumsum(live_rows) - live_rows
     stacked = jnp.stack([right_side, initial])
-    gathered = lax.all_gather(stacked, "fold", axis=2, tiled=True)
+    parts_n = lax.axis_size("fold")
+    leaves = tuple(((d, (d + 1) % parts_n) for d in range(parts_n)))
+    so_far_all = tuple(((src_i, b) for b, src_i in leaves))
+    current_block, new = ([], [])
+    for it in range(parts_n - 1):
+        if it % 2 == 0:
+            current_block.append(
+                lax.ppermute(current_block[-1] if current_block else stacked, "fold", leaves)
+            )
+        else:
+            new.append(lax.ppermute(new[-1] if new else stacked, "fold", so_far_all))
+    later = jnp.stack([*current_block[::-1], stacked, *new])
+    kept_arr = lax.axis_index("fold") - len(current_block)
+    later = later[(jnp.arange(parts_n) - kept_arr) % parts_n]
+    gathered = pack_panels_by_axis(later, 2)
     position = lax.axis_index("fold")
     row_ids = jnp.arange(own_blocks * width, dtype=jnp.int32)
     covered = starts[None, :] <= row_ids[:, None]

time: 566 us -> 560 us (0.989)
  between operations: 16.6 us -> 3.39 us
  starting transfers between devices: 100 us -> 108 us
  waiting for transfers between devices: 38.7 us -> 32.1 us
    all_gather x1 -> x0, waiting for transfers between devices: 24.7 us -> none  [on_device(): gathered = lax.all_gather(stacked, 'fold', axis=2, tiled=True)]
    all_gather x1 -> x0, local copies, waits for them, and re-layouts: 18.6 us -> none  [on_device(): gathered = lax.all_gather(stacked, 'fold', axis=2, tiled=True)]
    ppermute x0 -> x7, waiting for transfers between devices: none -> 18 us  [the longest x4 18 us: on_device(): lax.ppermute(current_block[-1] if current_block else stacked, 'fold', lea...]
    reshape x0 -> x1, local copies, waits for them, and re-layouts: none -> 16.6 us  [pack_panels_by_axis(): a0.reshape(*q_next[:array_dim], q_next[array_dim] * q_next[array_dim + 1]...]
    ppermute x0 -> x7, starting transfers between devices: none -> 8.14 us  [the longest x3 8.13 us: on_device(): new.append(lax.ppermute(new[-1] if new else stacked, 'fold', so_far_all))]
  transfers between devices with their start and end apart: 25 -> 31, of which waited for: 12 -> 15; matrix products, arithmetic and copies ran while one was open for 1% -> 2% of each run, Pallas kernels for 0% -> 0%
where the time goes in v1:
time: 560 us; the launch traced here: 554 us
  matrix products  278 us (50%)
  local copies, waits for them, and re-layouts  120 us (21%)
  starting transfers between devices  108 us (19%)
  waiting for transfers between devices  32.1 us (6%)
  other arithmetic  11.7 us (2%)
    dot_general x12, matrix products, operate(): jnp.einsum('nikc,ikrc->nir', picked, blocks, precision=lax.Precision.HIGH...  278 us
    gather x2, local copies, waits for them, and re-layouts, on_device(): owned = jnp.take(gathered, source, axis=2)  71.7 us
    ppermute x12, starting transfers between devices, padded_2(): after = lax.ppermute(initial, axis, down)  55.3 us
    ppermute x12, starting transfers between devices, padded_2(): before = lax.ppermute(last, axis, up)  45 us
    gather x12, local copies, waits for them, and re-layouts, operate(): picked = jnp.take(extended, columns, axis=1)  22.7 us
    ppermute x4, waiting for transfers between devices, on_device(): lax.ppermute(current_block[-1] if current_block else stacked, 'fold', lea...  18 us
    reshape x1, local copies, waits for them, and re-layouts, pack_panels_by_axis(): a0.reshape(*q_next[:array_dim], q_next[array_dim] * q_next[array_dim + 1]...  16.6 us
    ppermute x12, waiting for transfers between devices, padded_2(): after = lax.ppermute(initial, axis, down)  14 us
  transfers between devices with their start and end apart: 31, of which 15 were waited for; matrix products, arithmetic and copies ran while one was open for 2% of the time, Pallas kernels for 0%

profile of v1, /device:TPU:8, one launch (start us, length us, event | category | flops | bytes accessed | tf_op | source)
XLA Modules:
  0.0 553.8 jit_solution(13589345400071892902)
XLA Ops:
  5.6 4.6 collective-permute-done
  11.6 5.6 %collective-permute-done.1 = f32[2,16,2048]{2,1,0:T(8,128)S(1)} collective-permute-done((f32[2,16,2048]{2,1,0:T(8,128)S(1)}, f32[2,16,2048]{2,1,0:T(8,128)S(1)}, u32[]{:S(2)}, u32[]{:S(2)}) %collective-permute-start.1) | collective-permute-done | bytes 262176 | tf_op jit(solution)/shard_map/ppermute | solution.py:49
  39.5 16.6 %copy.369 = f32[2,16,8,2048]{1,0,3,2:T(2,128)} copy(f32[2,16,8,2048]{3,1,0,2:T(8,128)S(1)} %bitcast.366) | data formatting | bytes 4194304 | tf_op jit(solution)/shard_map/reshape | solution.py:16
  56.1 62.4 %gather_fusion.1 = f32[8192,2,16]{2,1,0:T(2,128)} fusion(f32[2,16,16384]{1,0,2:T(2,128)} %bitcast.365, s32[8192]{0:T(1024)S(1)} %broadcast_clamp_fusion), kind=kCustom, calls=%fused_computation.13 | custom fusion | bytes 2129920 | tf_op jit(solution)/shard_map/jit(_take)/gather | solution.py:63
  118.4 9.3 %copy.308 = f32[8192,2,16]{0,2,1:T(8,128)S(1)} copy(f32[8192,2,16]{2,1,0:T(2,128)} %gather_fusion.1) | data formatting | bytes 2097152 | tf_op jit(solution)/shard_map/jit(_take)/gather | solution.py:63
  139.4 23.1 %fusion.60 = f32[64,2,8,128]{3,2,1,0:T(8,128)S(1)} fusion(f32[64,5,128,128]{3,2,1,0:T(8,128)} %param.11, f32[64,5,16,128]{3,2,1,0:T(8,128)S(1)} %bitcast.354, pred[64,5]{1,0:T(8,128)(4,1)S(1)} %copy.309), kind=kOutput, calls=%fused_computation.74 | convolution fusion | flops 1007288320 | bytes 24117568 | tf_op jit(solution)/shard_map/nikc,ikrc->nir/dot_general | solution.py:71
  167.3 4.6 collective-permute-start.10
  175.1 23.1 %fusion.63 = f32[64,2,8,128]{3,2,1,0:T(8,128)S(1)} fusion(f32[64,5,128,128]{3,2,1,0:T(8,128)} %param.11, f32[64,5,16,128]{3,2,1,0:T(8,128)S(1)} %bitcast.355, pred[64,5]{1,0:T(8,128)(4,1)S(1)} %copy.309), kind=kOutput, calls=%fused_computation.75 | convolution fusion | flops 1007288320 | bytes 24117568 | tf_op jit(solution)/shard_map/nikc,ikrc->nir/dot_general | solution.py:71
  210.1 23.1 %fusion.66 = f32[64,2,8,128]{3,2,1,0:T(8,128)S(1)} fusion(f32[64,5,128,128]{3,2,1,0:T(8,128)} %param.11, f32[64,5,16,128]{3,2,1,0:T(8,128)S(1)} %bitcast.356, pred[64,5]{1,0:T(8,128)(4,1)S(1)} %copy.309), kind=kOutput, calls=%fused_computation.76 | convolution fusion | flops 1007288320 | bytes 24117568 | tf_op jit(solution)/shard_map/nikc,ikrc->nir/dot_general | solution.py:71
  237.2 5.0 collective-permute-start.14
  245.2 23.2 %fusion.69 = f32[64,2,8,128]{3,2,1,0:T(8,128)S(1)} fusion(f32[64,5,128,128]{3,2,1,0:T(8,128)} %param.11, f32[64,5,16,128]{3,2,1,0:T(8,128)S(1)} %bitcast.357, pred[64,5]{1,0:T(8,128)(4,1)S(1)} %copy.309), kind=kOutput, calls=%fused_computation.77 | convolution fusion | flops 1007288320 | bytes 24117568 | tf_op jit(solution)/shard_map/nikc,ikrc->nir/dot_general | solution.py:71
  280.5 23.1 %fusion.72 = f32[64,2,8,128]{3,2,1,0:T(8,128)S(1)} fusion(f32[64,5,128,128]{3,2,1,0:T(8,128)} %param.11, f32[64,5,16,128]{3,2,1,0:T(8,128)S(1)} %bitcast.358, pred[64,5]{1,0:T(8,128)(4,1)S(1)} %copy.309), kind=kOutput, calls=%fused_computation.78 | convolution fusion | flops 1007288320 | bytes 24117568 | tf_op jit(solution)/shard_map/nikc,ikrc->nir/dot_general | solution.py:71
  308.3 4.7 collective-permute-start.18
  316.2 23.1 %fusion.75 = f32[64,2,8,128]{3,2,1,0:T(8,128)S(1)} fusion(f32[64,5,128,128]{3,2,1,0:T(8,128)} %param.11, f32[64,5,16,128]{3,2,1,0:T(8,128)S(1)} %bitcast.359, pred[64,5]{1,0:T(8,128)(4,1)S(1)} %copy.309), kind=kOutput, calls=%fused_computation.79 | convolution fusion | flops 1007288320 | bytes 24117568 | tf_op jit(solution)/shard_map/nikc,ikrc->nir/dot_general | solution.py:71
  351.2 23.1 %fusion.78 = f32[64,2,8,128]{3,2,1,0:T(8,128)S(1)} fusion(f32[64,5,128,128]{3,2,1,0:T(8,128)} %param.11, f32[64,5,16,128]{3,2,1,0:T(8,128)S(1)} %bitcast.360, pred[64,5]{1,0:T(8,128)(4,1)S(1)} %copy.309), kind=kOutput, calls=%fused_computation.80 | convolution fusion | flops 1007288320 | bytes 24117568 | tf_op jit(solution)/shard_map/nikc,ikrc->nir/dot_general | solution.py:71
  378.3 4.7 collective-permute-start.22
  386.3 23.2 %fusion.81 = f32[64,2,8,128]{3,2,1,0:T(8,128)S(1)} fusion(f32[64,5,128,128]{3,2,1,0:T(8,128)} %param.11, f32[64,5,16,128]{3,2,1,0:T(8,128)S(1)} %bitcast.361, pred[64,5]{1,0:T(8,128)(4,1)S(1)} %copy.309), kind=kOutput, calls=%fused_computation.81 | convolution fusion | flops 1007288320 | bytes 24117568 | tf_op jit(solution)/shard_map/nikc,ikrc->nir/dot_general | solution.py:71
  413.6 4.5 collective-permute-start.24
  421.6 23.1 %fusion.84 = f32[64,2,8,128]{3,2,1,0:T(8,128)S(1)} fusion(f32[64,5,128,128]{3,2,1,0:T(8,128)} %param.11, f32[64,5,16,128]{3,2,1,0:T(8,128)S(1)} %bitcast.362, pred[64,5]{1,0:T(8,128)(4,1)S(1)} %copy.309), kind=kOutput, calls=%fused_computation.82 | convolution fusion | flops 1007288320 | bytes 24117568 | tf_op jit(solution)/shard_map/nikc,ikrc->nir/dot_general | solution.py:71
  449.4 4.9 collective-permute-start.26
  457.4 23.1 %fusion.87 = f32[64,2,8,128]{3,2,1,0:T(8,128)S(1)} fusion(f32[64,5,128,128]{3,2,1,0:T(8,128)} %param.11, f32[64,5,16,128]{3,2,1,0:T(8,128)S(1)} %bitcast.363, pred[64,5]{1,0:T(8,128)(4,1)S(1)} %copy.309), kind=kOutput, calls=%fused_computation.83 | convolution fusion | flops 1007288320 | bytes 24117568 | tf_op jit(solution)/shard_map/nikc,ikrc->nir/dot_general | solution.py:71
  492.4 23.1 %fusion.90 = f32[64,2,8,128]{3,2,1,0:T(8,128)S(1)} fusion(f32[64,5,128,128]{3,2,1,0:T(8,128)} %param.11, f32[64,5,16,128]{3,2,1,0:T(8,128)S(1)} %bitcast.364, pred[64,5]{1,0:T(8,128)(4,1)S(1)} %copy.309), kind=kOutput, calls=%fused_computation.84 | convolution fusion | flops 1007288320 | bytes 24117568 | tf_op jit(solution)/shard_map/nikc,ikrc->nir/dot_general | solution.py:71
  520.1 4.7 collective-permute-start.30
  529.3 23.2 %fusion.93 = f32[64,2,8,128]{3,2,1,0:T(8,128)S(1)} fusion(f32[64,5,128,128]{3,2,1,0:T(8,128)} %param.11, f32[64,5,16,128]{3,2,1,0:T(8,128)S(1)} %bitcast.353, pred[64,5]{1,0:T(8,128)(4,1)S(1)} %copy.309), kind=kOutput, calls=%fused_computation.85 | convolution fusion | flops 1007288320 | bytes 24117568 | tf_op jit(solution)/shard_map/nikc,ikrc->nir/dot_general | solution.py:71
  (225 shorter events, 141.1 us)
Async XLA Ops:
  1.0 16.3 %collective-permute-start.4 = (f32[2,16,2048]{2,1,0:T(8,128)S(1)}, f32[2,16,2048]{2,1,0:T(8,128)S(1)}, u32[]{:S(2)}, u32[]{:S(2)}) collective-permute-start(f32[2,16,2048]{2,1,0:T(8,128)S(1)} %pad_maximum_fusion), channel_id=1, source_target_pairs={{1,0},{2,1},{3,2},{4,3},{5,4},{6,5},{7,6},{0,7},{9,8},{10,9},{11,1... | collective-permute-start | bytes 786440 | tf_op jit(solution)/shard_map/ppermute | solution.py:52
  3.2 7.0 %collective-permute-start = (f32[2,16,2048]{2,1,0:T(8,128)S(1)}, f32[2,16,2048]{2,1,0:T(8,128)S(1)}, u32[]{:S(2)}, u32[]{:S(2)}) collective-permute-start(f32[2,16,2048]{2,1,0:T(8,128)S(1)} %pad_maximum_fusion), channel_id=1, source_target_pairs={{0,1},{1,2},{2,3},{3,4},{4,5},{5,6},{6,7},{7,0},{8,9},{9,10},{10,1... | collective-permute-start | bytes 786440 | tf_op jit(solution)/shard_map/ppermute | solution.py:49
  10.3 7.0 %collective-permute-start.1 = (f32[2,16,2048]{2,1,0:T(8,128)S(1)}, f32[2,16,2048]{2,1,0:T(8,128)S(1)}, u32[]{:S(2)}, u32[]{:S(2)}) collective-permute-start(f32[2,16,2048]{2,1,0:T(8,128)S(1)} %collective-permute-done), channel_id=1, source_target_pairs={{0,1},{1,2},{2,3},{3,4},{4,5},{5,6},{6,7},{7,0},{8,9},{9,10},{10,1... | collective-permute-start | bytes 786440 | tf_op jit(solution)/shard_map/ppermute | solution.py:49
  17.3 7.0 %collective-permute-start.2 = (f32[2,16,2048]{2,1,0:T(8,128)S(1)}, f32[2,16,2048]{2,1,0:T(8,128)S(1)}, u32[]{:S(2)}, u32[]{:S(2)}) collective-permute-start(f32[2,16,2048]{2,1,0:T(8,128)S(1)} %collective-permute-done.1), channel_id=1, source_target_pairs={{0,1},{1,2},{2,3},{3,4},{4,5},{5,6},{6,7},{7,0},{8,9},{9,10},{10,1... | collective-permute-start | bytes 786440 | tf_op jit(solution)/shard_map/ppermute | solution.py:49
  17.3 7.2 %collective-permute-start.5 = (f32[2,16,2048]{2,1,0:T(8,128)S(1)}, f32[2,16,2048]{2,1,0:T(8,128)S(1)}, u32[]{:S(2)}, u32[]{:S(2)}) collective-permute-start(f32[2,16,2048]{2,1,0:T(8,128)S(1)} %collective-permute-done.4), channel_id=1, source_target_pairs={{1,0},{2,1},{3,2},{4,3},{5,4},{6,5},{7,6},{0,7},{9,8},{10,9},{11,1... | collective-permute-start | bytes 786440 | tf_op jit(solution)/shard_map/ppermute | solution.py:52
  24.3 7.0 %collective-permute-start.3 = (f32[2,16,2048]{2,1,0:T(8,128)S(1)}, f32[2,16,2048]{2,1,0:T(8,128)S(1)}, u32[]{:S(2)}, u32[]{:S(2)}) collective-permute-start(f32[2,16,2048]{2,1,0:T(8,128)S(1)} %collective-permute-done.2), channel_id=1, source_target_pairs={{0,1},{1,2},{2,3},{3,4},{4,5},{5,6},{6,7},{7,0},{8,9},{9,10},{10,1... | collective-permute-start | bytes 786440 | tf_op jit(solution)/shard_map/ppermute | solution.py:49
  24.6 11.9 %collective-permute-start.6 = (f32[2,16,2048]{2,1,0:T(8,128)S(1)}, f32[2,16,2048]{2,1,0:T(8,128)S(1)}, u32[]{:S(2)}, u32[]{:S(2)}) collective-permute-start(f32[2,16,2048]{2,1,0:T(8,128)S(1)} %collective-permute-done.5), channel_id=1, source_target_pairs={{1,0},{2,1},{3,2},{4,3},{5,4},{6,5},{7,6},{0,7},{9,8},{10,9},{11,1... | collective-permute-start | bytes 786440 | tf_op jit(solution)/shard_map/ppermute | solution.py:52
  127.9 8.1 %collective-permute-start.7 = (f32[16,384]{1,0:T(8,128)S(1)}, f32[16,384]{1,0:T(8,128)S(1)}, u32[]{:S(2)}, u32[]{:S(2)}) collective-permute-start(f32[16,384]{1,0:T(8,128)S(1)} %get-tuple-element.38), channel_id=1, source_target_pairs={{0,8},{8,16},{16,24},{24,32},{32,40},{40,48},{48,56},{56,64},{64,7... | collective-permute-start | bytes 73736 | tf_op jit(solution)/shard_map/ppermute | solution.py:29
  163.5 8.5 %collective-permute-start.9 = (f32[16,384]{1,0:T(8,128)S(1)}, f32[16,384]{1,0:T(8,128)S(1)}, u32[]{:S(2)}, u32[]{:S(2)}) collective-permute-start(f32[16,384]{1,0:T(8,128)S(1)} %get-tuple-element.36), channel_id=1, source_target_pairs={{0,8},{8,16},{16,24},{24,32},{32,40},{40,48},{48,56},{56,64},{64,7... | collective-permute-start | bytes 73736 | tf_op jit(solution)/shard_map/ppermute | solution.py:29
  198.4 8.3 %collective-permute-start.11 = (f32[16,384]{1,0:T(8,128)S(1)}, f32[16,384]{1,0:T(8,128)S(1)}, u32[]{:S(2)}, u32[]{:S(2)}) collective-permute-start(f32[16,384]{1,0:T(8,128)S(1)} %get-tuple-element.34), channel_id=1, source_target_pairs={{0,8},{8,16},{16,24},{24,32},{32,40},{40,48},{48,56},{56,64},{64,7... | collective-permute-start | bytes 73736 | tf_op jit(solution)/shard_map/ppermute | solution.py:29
  202.1 6.0 %collective-permute-start.12 = (f32[16,384]{1,0:T(8,128)S(1)}, f32[16,384]{1,0:T(8,128)S(1)}, u32[]{:S(2)}, u32[]{:S(2)}) collective-permute-start(f32[16,384]{1,0:T(8,128)S(1)} %get-tuple-element.35), channel_id=1, source_target_pairs={{8,0},{16,8},{24,16},{32,24},{40,32},{48,40},{56,48},{64,56},{72,6... | collective-permute-start | bytes 73736 | tf_op jit(solution)/shard_map/ppermute | solution.py:30
  233.4 8.8 %collective-permute-start.13 = (f32[16,384]{1,0:T(8,128)S(1)}, f32[16,384]{1,0:T(8,128)S(1)}, u32[]{:S(2)}, u32[]{:S(2)}) collective-permute-start(f32[16,384]{1,0:T(8,128)S(1)} %get-tuple-element.32), channel_id=1, source_target_pairs={{0,8},{8,16},{16,24},{24,32},{32,40},{40,48},{48,56},{56,64},{64,7... | collective-permute-start | bytes 73736 | tf_op jit(solution)/shard_map/ppermute | solution.py:29
  237.2 6.0 %collective-permute-start.14 = (f32[16,384]{1,0:T(8,128)S(1)}, f32[16,384]{1,0:T(8,128)S(1)}, u32[]{:S(2)}, u32[]{:S(2)}) collective-permute-start(f32[16,384]{1,0:T(8,128)S(1)} %get-tuple-element.33), channel_id=1, source_target_pairs={{8,0},{16,8},{24,16},{32,24},{40,32},{48,40},{56,48},{64,56},{72,6... | collective-permute-start | bytes 73736 | tf_op jit(solution)/shard_map/ppermute | solution.py:30
  268.8 8.3 %collective-permute-start.15 = (f32[16,384]{1,0:T(8,128)S(1)}, f32[16,384]{1,0:T(8,128)S(1)}, u32[]{:S(2)}, u32[]{:S(2)}) collective-permute-start(f32[16,384]{1,0:T(8,128)S(1)} %get-tuple-element.30), channel_id=1, source_target_pairs={{0,8},{8,16},{16,24},{24,32},{32,40},{40,48},{48,56},{56,64},{64,7... | collective-permute-start | bytes 73736 | tf_op jit(solution)/shard_map/ppermute | solution.py:29
  304.5 8.4 %collective-permute-start.17 = (f32[16,384]{1,0:T(8,128)S(1)}, f32[16,384]{1,0:T(8,128)S(1)}, u32[]{:S(2)}, u32[]{:S(2)}) collective-permute-start(f32[16,384]{1,0:T(8,128)S(1)} %get-tuple-element.28), channel_id=1, source_target_pairs={{0,8},{8,16},{16,24},{24,32},{32,40},{40,48},{48,56},{56,64},{64,7... | collective-permute-start | bytes 73736 | tf_op jit(solution)/shard_map/ppermute | solution.py:29
  308.3 6.0 %collective-permute-start.18 = (f32[16,384]{1,0:T(8,128)S(1)}, f32[16,384]{1,0:T(8,128)S(1)}, u32[]{:S(2)}, u32[]{:S(2)}) collective-permute-start(f32[16,384]{1,0:T(8,128)S(1)} %get-tuple-element.29), channel_id=1, source_target_pairs={{8,0},{16,8},{24,16},{32,24},{40,32},{48,40},{56,48},{64,56},{72,6... | collective-permute-start | bytes 73736 | tf_op jit(solution)/shard_map/ppermute | solution.py:30
  339.5 8.3 %collective-permute-start.19 = (f32[16,384]{1,0:T(8,128)S(1)}, f32[16,384]{1,0:T(8,128)S(1)}, u32[]{:S(2)}, u32[]{:S(2)}) collective-permute-start(f32[16,384]{1,0:T(8,128)S(1)} %get-tuple-element.26), channel_id=1, source_target_pairs={{0,8},{8,16},{16,24},{24,32},{32,40},{40,48},{48,56},{56,64},{64,7... | collective-permute-start | bytes 73736 | tf_op jit(solution)/shard_map/ppermute | solution.py:29
  374.6 8.5 %collective-permute-start.21 = (f32[16,384]{1,0:T(8,128)S(1)}, f32[16,384]{1,0:T(8,128)S(1)}, u32[]{:S(2)}, u32[]{:S(2)}) collective-permute-start(f32[16,384]{1,0:T(8,128)S(1)} %get-tuple-element.24), channel_id=1, source_target_pairs={{0,8},{8,16},{16,24},{24,32},{32,40},{40,48},{48,56},{56,64},{64,7... | collective-permute-start | bytes 73736 | tf_op jit(solution)/shard_map/ppermute | solution.py:29
  409.9 8.3 %collective-permute-start.23 = (f32[16,384]{1,0:T(8,128)S(1)}, f32[16,384]{1,0:T(8,128)S(1)}, u32[]{:S(2)}, u32[]{:S(2)}) collective-permute-start(f32[16,384]{1,0:T(8,128)S(1)} %get-tuple-element.22), channel_id=1, source_target_pairs={{0,8},{8,16},{16,24},{24,32},{32,40},{40,48},{48,56},{56,64},{64,7... | collective-permute-start | bytes 73736 | tf_op jit(solution)/shard_map/ppermute | solution.py:29
  445.7 8.7 %collective-permute-start.25 = (f32[16,384]{1,0:T(8,128)S(1)}, f32[16,384]{1,0:T(8,128)S(1)}, u32[]{:S(2)}, u32[]{:S(2)}) collective-permute-start(f32[16,384]{1,0:T(8,128)S(1)} %get-tuple-element.20), channel_id=1, source_target_pairs={{0,8},{8,16},{16,24},{24,32},{32,40},{40,48},{48,56},{56,64},{64,7... | collective-permute-start | bytes 73736 | tf_op jit(solution)/shard_map/ppermute | solution.py:29
  449.4 6.0 %collective-permute-start.26 = (f32[16,384]{1,0:T(8,128)S(1)}, f32[16,384]{1,0:T(8,128)S(1)}, u32[]{:S(2)}, u32[]{:S(2)}) collective-permute-start(f32[16,384]{1,0:T(8,128)S(1)} %get-tuple-element.21), channel_id=1, source_target_pairs={{8,0},{16,8},{24,16},{32,24},{40,32},{48,40},{56,48},{64,56},{72,6... | collective-permute-start | bytes 73736 | tf_op jit(solution)/shard_map/ppermute | solution.py:30
  480.6 9.0 %collective-permute-start.27 = (f32[16,384]{1,0:T(8,128)S(1)}, f32[16,384]{1,0:T(8,128)S(1)}, u32[]{:S(2)}, u32[]{:S(2)}) collective-permute-start(f32[16,384]{1,0:T(8,128)S(1)} %get-tuple-element.18), channel_id=1, source_target_pairs={{0,8},{8,16},{16,24},{24,32},{32,40},{40,48},{48,56},{56,64},{64,7... | collective-permute-start | bytes 73736 | tf_op jit(solution)/shard_map/ppermute | solution.py:29
  516.4 10.9 %collective-permute-start.29 = (f32[16,384]{1,0:T(8,128)S(1)}, f32[16,384]{1,0:T(8,128)S(1)}, u32[]{:S(2)}, u32[]{:S(2)}) collective-permute-start(f32[16,384]{1,0:T(8,128)S(1)} %get-tuple-element.16), channel_id=1, source_target_pairs={{0,8},{8,16},{16,24},{24,32},{32,40},{40,48},{48,56},{56,64},{64,7... | collective-permute-start | bytes 73736 | tf_op jit(solution)/shard_map/ppermute | solution.py:29
  520.1 7.2 %collective-permute-start.30 = (f32[16,384]{1,0:T(8,128)S(1)}, f32[16,384]{1,0:T(8,128)S(1)}, u32[]{:S(2)}, u32[]{:S(2)}) collective-permute-start(f32[16,384]{1,0:T(8,128)S(1)} %get-tuple-element.17), channel_id=1, source_target_pairs={{8,0},{16,8},{24,16},{32,24},{40,32},{48,40},{56,48},{64,56},{72,6... | collective-permute-start | bytes 73736 | tf_op jit(solution)/shard_map/ppermute | solution.py:30
  (54 other events, 973.5 us)
